TPU v7x, 32 devices: a whole 2x2x4 slice. The times are simulated.
32 devices in a mesh: batch: 16 (over z, y, x), mp: 2 (over core).
Axes of the slice: x: 2, y: 2, z: 4, core: 2. Of those that a mesh axis runs over, the one named last changes fastest.
Arguments:
- hidden: bfloat16 [16384, 1024], P(('batch', 'mp')), may hold values from -6 to 6
- cell_ids: int32 [32, 512], P('batch'), may hold values from 0 to 127, never falling along the last dimension, each value on 1 to 60 neighbouring positions
- boxes: int32 [32, 128, 4], P('batch'), may hold values from 0 to 1023
- x_table: bfloat16 [1024, 1024], replicated, may hold values from -3 to 3
- y_table: bfloat16 [1024, 1024], replicated, may hold values from -3 to 3
- w_query: bfloat16 [1024, 1024], P(None, 'mp'), may hold values from -0.1875 to 0.1875
- b_query: bfloat16 [1024], P('mp'), may hold values from -3 to 3
- w_key: bfloat16 [1024, 1024], P(None, 'mp'), may hold values from -0.1875 to 0.1875
- w_value: bfloat16 [1024, 1024], P(None, 'mp'), may hold values from -0.1875 to 0.1875
- b_value: bfloat16 [1024], P('mp'), may hold values from -3 to 3
- w_out: bfloat16 [1024, 1024], P('mp'), may hold values from -3 to 3
- b_out: bfloat16 [1024], replicated, may hold values from -3 to 3
- ln1_gain: bfloat16 [1024], replicated, may hold values from 0.5 to 1.5
- ln1_bias: bfloat16 [1024], replicated, may hold values from -1 to 1
- w_up: bfloat16 [1024, 4096], P(None, 'mp'), may hold values from -0.1875 to 0.1875
- b_up: bfloat16 [4096], P('mp'), may hold values from -3 to 3
- w_down: bfloat16 [4096, 1024], P('mp'), may hold values from -0.09375 to 0.09375
- b_down: bfloat16 [1024], replicated, may hold values from -3 to 3
- ln2_gain: bfloat16 [1024], replicated, may hold values from 0.5 to 1.5
- ln2_bias: bfloat16 [1024], replicated, may hold values from -1 to 1
- d_out: bfloat16 [16384, 1024], P(('batch', 'mp')), may hold values from -6 to 6
Outputs:
- layer_out: bfloat16 [16384, 1024], P(('batch', 'mp'))
- d_hidden: float32 [16384, 1024], P(('batch', 'mp'))
- grad_w_query: float32 [1024, 1024], P(None, 'mp')
- grad_b_query: float32 [1024], P('mp')
- grad_w_key: float32 [1024, 1024], P(None, 'mp')
- grad_w_value: float32 [1024, 1024], P(None, 'mp')
- grad_b_value: float32 [1024], P('mp')
- grad_w_out: float32 [1024, 1024], P('mp')
- grad_b_out: float32 [1024], replicated
- grad_ln1_gain: float32 [1024], replicated
- grad_ln1_bias: float32 [1024], replicated
- grad_w_up: float32 [1024, 4096], P(None, 'mp')
- grad_b_up: float32 [4096], P('mp')
- grad_w_down: float32 [4096, 1024], P('mp')
- grad_b_down: float32 [1024], replicated
- grad_ln2_gain: float32 [1024], replicated
- grad_ln2_bias: float32 [1024], replicated
Inputs may be any that keep to these rules, and one draw needn't show every extreme that they name: `cell_ids`: numbered from 0 within each page, never falling along a page; each of the 128 cells has 1 to 60 tokens and one has 60.
All inputs are finite; a program needn't handle non-finite values.
Results may differ from a plain program's by a relative error of at most 0.023.
Values may be sent and summed in bfloat16 or wider, within the bound.
No kernel may reach another device: no remote copies, remote signals or barrier semaphores. Data moves between devices by JAX's collectives and lax.ppermute only.
A program may use at most 128 MiB of HBM per device.

v0:
```python
import jax
import jax.numpy as jnp
from jax import lax
from jax.sharding import PartitionSpec as P

HDIM = 64
PAGE_LEN = 512
CELLS = 128


def contract_rows(left, right):
    return lax.dot_general(
        left, right, (((0,), (0,)), ((), ())), preferred_element_type=jnp.float32
    )


def contract_last(left, right):
    return lax.dot_general(
        left, right, (((1,), (1,)), ((), ())), preferred_element_type=jnp.float32
    )


def layer_norm(values, gain, shift):
    average = jnp.mean(values, axis=-1, keepdims=True)
    centred = values - average
    rstd_rows = lax.rsqrt(jnp.mean(centred * centred, axis=-1, keepdims=True) + 1e-12)
    normed = centred * rstd_rows
    return (normed * gain + shift, normed, rstd_rows)


def norm_back(upstream, normed, rstd_rows, gain):
    scaled = upstream * gain
    return rstd_rows * (
        scaled
        - jnp.mean(scaled, axis=-1, keepdims=True)
        - normed * jnp.mean(scaled * normed, axis=-1, keepdims=True)
    )


def gelu_slope(values):
    return (
        0.5 * (1.0 + lax.erf(values * 0.7071067811865476))
        + values * jnp.exp(-0.5 * values * values) * 0.3989422804014327
    )


def page_scores(queries, keys_page):
    return jnp.einsum(
        "qhd,khd->hqk", queries, keys_page, preferred_element_type=jnp.float32
    ) * HDIM ** (-0.5)


def attend(page_block):
    queries, keys_page, values_page = page_block
    scores = page_scores(queries, keys_page)
    maximum = jnp.max(scores, axis=-1, keepdims=True)
    log_total = maximum + jnp.log(jnp.sum(jnp.exp(scores - maximum), axis=-1, keepdims=True))
    weights = jnp.exp(scores - log_total).astype(jnp.bfloat16)
    context = jnp.einsum("hqk,khd->qhd", weights, values_page, preferred_element_type=jnp.float32)
    return (context.astype(jnp.bfloat16), log_total[..., 0])


def attend_back(page_block):
    queries, keys_page, values_page, log_total, d_context = page_block
    weights = jnp.exp(page_scores(queries, keys_page) - log_total[..., None])
    d_weights = jnp.einsum(
        "qhd,khd->hqk", d_context, values_page, preferred_element_type=jnp.float32
    )
    d_values = jnp.einsum(
        "hqk,qhd->khd", weights.astype(jnp.bfloat16), d_context, preferred_element_type=jnp.float32
    )
    d_scores = (
        weights * (d_weights - jnp.sum(weights * d_weights, axis=-1, keepdims=True))
    ).astype(jnp.bfloat16)
    factor = HDIM ** (-0.5)
    d_queries = (
        jnp.einsum("hqk,khd->qhd", d_scores, keys_page, preferred_element_type=jnp.float32) * factor
    )
    d_keys = (
        jnp.einsum("hqk,qhd->khd", d_scores, queries, preferred_element_type=jnp.float32) * factor
    )
    return (
        d_queries.astype(jnp.bfloat16),
        d_keys.astype(jnp.bfloat16),
        d_values.astype(jnp.bfloat16),
    )


def shards(
    hidden,
    cell_ids,
    boxes,
    x_table,
    y_table,
    w_query,
    b_query,
    w_key,
    w_value,
    b_value,
    w_out,
    b_out,
    ln1_gain,
    ln1_bias,
    w_up,
    b_up,
    w_down,
    b_down,
    ln2_gain,
    ln2_bias,
    d_out,
):
    row_count = hidden.shape[0]
    width_local = w_query.shape[1]
    first_row = lax.axis_index("mp") * row_count
    own_cells = lax.dynamic_slice_in_dim(cell_ids.reshape(-1), first_row, row_count)
    page_local = (first_row + jnp.arange(row_count, dtype=jnp.int32)) // PAGE_LEN
    cell_boxes = jnp.take(boxes.reshape(-1, 4), page_local * CELLS + own_cells, axis=0)
    layout = (
        jnp.take(x_table, cell_boxes[:, 0], axis=0).astype(jnp.float32)
        + jnp.take(y_table, cell_boxes[:, 1], axis=0).astype(jnp.float32)
        + jnp.take(x_table, cell_boxes[:, 2], axis=0).astype(jnp.float32)
        + jnp.take(y_table, cell_boxes[:, 3], axis=0).astype(jnp.float32)
    )
    inputs = hidden.astype(jnp.float32) + layout
    x_all = lax.all_gather(inputs.astype(jnp.bfloat16), "mp", axis=0, tiled=True)
    queries = (
        jnp.dot(x_all, w_query, preferred_element_type=jnp.float32) + b_query.astype(jnp.float32)
    ).astype(jnp.bfloat16)
    keys_all = jnp.dot(x_all, w_key, preferred_element_type=jnp.float32).astype(jnp.bfloat16)
    values_all = (
        jnp.dot(x_all, w_value, preferred_element_type=jnp.float32) + b_value.astype(jnp.float32)
    ).astype(jnp.bfloat16)
    page_shape = (-1, PAGE_LEN, width_local // HDIM, HDIM)
    page_split = (
        queries.reshape(page_shape),
        keys_all.reshape(page_shape),
        values_all.reshape(page_shape),
    )
    context, log_total = lax.map(attend, page_split)
    context = context.reshape(-1, width_local)
    attn_rows = lax.psum_scatter(
        jnp.dot(context, w_out, preferred_element_type=jnp.float32),
        "mp",
        scatter_dimension=0,
        tiled=True,
    )
    resid = inputs + attn_rows + b_out.astype(jnp.float32)
    hidden_mid, normed_one, rstd_one = layer_norm(
        resid, ln1_gain.astype(jnp.float32), ln1_bias.astype(jnp.float32)
    )
    mid_low = hidden_mid.astype(jnp.bfloat16)
    mid_all = lax.all_gather(mid_low, "mp", axis=0, tiled=True)
    pre_act = jnp.dot(mid_all, w_up, preferred_element_type=jnp.float32) + b_up.astype(jnp.float32)
    activ = jax.nn.gelu(pre_act, approximate=False).astype(jnp.bfloat16)
    ffn_rows = lax.psum_scatter(
        jnp.dot(activ, w_down, preferred_element_type=jnp.float32),
        "mp",
        scatter_dimension=0,
        tiled=True,
    )
    second = hidden_mid + ffn_rows + b_down.astype(jnp.float32)
    final, normed_two, rstd_two = layer_norm(
        second, ln2_gain.astype(jnp.float32), ln2_bias.astype(jnp.float32)
    )
    layer_out = final.astype(jnp.bfloat16)
    upstream = d_out.astype(jnp.float32)
    grad_ln2_gain = jnp.sum(upstream * normed_two, axis=0)
    grad_ln2_bias = jnp.sum(upstream, axis=0)
    d_second = norm_back(upstream, normed_two, rstd_two, ln2_gain.astype(jnp.float32))
    grad_b_down = jnp.sum(d_second, axis=0)
    second_low = d_second.astype(jnp.bfloat16)
    grads_all = lax.all_gather(second_low, "mp", axis=0, tiled=True)
    grad_w_down = contract_rows(activ, grads_all)
    d_pre = (contract_last(grads_all, w_down) * gelu_slope(pre_act)).astype(jnp.bfloat16)
    grad_w_up = contract_rows(mid_all, d_pre)
    grad_b_up = jnp.sum(d_pre.astype(jnp.float32), axis=0)
    d_mid_ffn = lax.psum_scatter(contract_last(d_pre, w_up), "mp", scatter_dimension=0, tiled=True)
    d_mid = d_second + d_mid_ffn
    grad_ln1_gain = jnp.sum(d_mid * normed_one, axis=0)
    grad_ln1_bias = jnp.sum(d_mid, axis=0)
    d_resid = norm_back(d_mid, normed_one, rstd_one, ln1_gain.astype(jnp.float32))
    grad_b_out = jnp.sum(d_resid, axis=0)
    resid_all = lax.all_gather(d_resid.astype(jnp.bfloat16), "mp", axis=0, tiled=True)
    grad_w_out = contract_rows(context, resid_all)
    d_context = contract_last(resid_all, w_out).astype(jnp.bfloat16).reshape(page_shape)
    d_queries, d_keys, d_values = lax.map(attend_back, page_split + (log_total, d_context))
    d_queries = d_queries.reshape(-1, width_local)
    d_keys = d_keys.reshape(-1, width_local)
    d_values = d_values.reshape(-1, width_local)
    grad_w_query = contract_rows(x_all, d_queries)
    grad_w_key = contract_rows(x_all, d_keys)
    grad_w_value = contract_rows(x_all, d_values)
    grad_b_query = jnp.sum(d_queries.astype(jnp.float32), axis=0)
    grad_b_value = jnp.sum(d_values.astype(jnp.float32), axis=0)
    d_hidden = d_resid + lax.psum_scatter(
        (
            contract_last(d_queries, w_query)
            + contract_last(d_keys, w_key)
            + contract_last(d_values, w_value)
        ).astype(jnp.bfloat16),
        "mp",
        scatter_dimension=0,
        tiled=True,
    ).astype(jnp.float32)
    (
        grad_w_query,
        grad_b_query,
        grad_w_key,
        grad_w_value,
        grad_b_value,
        grad_w_out,
        grad_w_up,
        grad_b_up,
        grad_w_down,
    ) = (
        lax.psum(grad_w_query.astype(jnp.bfloat16), "batch").astype(jnp.float32),
        lax.psum(grad_b_query.astype(jnp.bfloat16), "batch").astype(jnp.float32),
        lax.psum(grad_w_key.astype(jnp.bfloat16), "batch").astype(jnp.float32),
        lax.psum(grad_w_value.astype(jnp.bfloat16), "batch").astype(jnp.float32),
        lax.psum(grad_b_value.astype(jnp.bfloat16), "batch").astype(jnp.float32),
        lax.psum(grad_w_out.astype(jnp.bfloat16), "batch").astype(jnp.float32),
        lax.psum(grad_w_up.astype(jnp.bfloat16), "batch").astype(jnp.float32),
        lax.psum(grad_b_up.astype(jnp.bfloat16), "batch").astype(jnp.float32),
        lax.psum(grad_w_down.astype(jnp.bfloat16), "batch").astype(jnp.float32),
    )
    grad_b_out, grad_ln1_gain, grad_ln1_bias, grad_b_down, grad_ln2_gain, grad_ln2_bias = lax.psum(
        (grad_b_out, grad_ln1_gain, grad_ln1_bias, grad_b_down, grad_ln2_gain, grad_ln2_bias),
        ("batch", "mp"),
    )
    return (
        layer_out,
        d_hidden,
        grad_w_query,
        grad_b_query,
        grad_w_key,
        grad_w_value,
        grad_b_value,
        grad_w_out,
        grad_b_out,
        grad_ln1_gain,
        grad_ln1_bias,
        grad_w_up,
        grad_b_up,
        grad_w_down,
        grad_b_down,
        grad_ln2_gain,
        grad_ln2_bias,
    )


def solution(mesh):
    in_specs = (
        P(("batch", "mp"), None),
        P("batch", None),
        P("batch", None, None),
        P(),
        P(),
        P(None, "mp"),
        P("mp"),
        P(None, "mp"),
        P(None, "mp"),
        P("mp"),
        P("mp", None),
        P(),
        P(),
        P(),
        P(None, "mp"),
        P("mp"),
        P("mp", None),
        P(),
        P(),
        P(),
        P(("batch", "mp"), None),
    )
    out_specs = (
        P(("batch", "mp"), None),
        P(("batch", "mp"), None),
        P(None, "mp"),
        P("mp"),
        P(None, "mp"),
        P(None, "mp"),
        P("mp"),
        P("mp", None),
        P(),
        P(),
        P(),
        P(None, "mp"),
        P("mp"),
        P("mp", None),
        P(),
        P(),
        P(),
    )
    return jax.shard_map(shards, mesh=mesh, in_specs=in_specs, out_specs=out_specs, check_vma=False)
```

profile of v0, /device:TPU:0, one launch (start us, length us, event | category | flops | bytes accessed | tf_op | source)
XLA Modules:
  0.0 700.1 jit_solution(8458839634089925012)
XLA Ops:
  10.9 2.1 gather_fusion.1
  12.9 2.8 gather_fusion.3
  15.7 5.5 gather_fusion.2
  21.2 2.8 gather_fusion.4
  24.0 4.1 fusion.92
  28.2 13.3 %all-gather.5.cloned.1.call-done = bf16[1024,1024]{1,0:T(8,128)(2,1)} async-done(((bf16[512,1024]{1,0:T(8,128)(2,1)}), bf16[1024,1024]{1,0:T(8,128)(2,1)}) %all-gather.5.cloned.1.call-update) | async-done | bytes 2097168 | tf_op jit(solution)/shard_map/all_gather | solution.py:125
  41.5 2.8 add_convert_fusion.3
  44.4 2.4 reshape.218
  46.7 2.5 copy.58
  49.2 3.1 add_convert_fusion.2
  52.3 2.1 reshape.219
  54.4 2.5 copy.59
  56.9 3.1 convolution_convert_fusion.7
  60.0 2.1 reshape.220
  62.1 2.5 copy.60
  65.7 10.6 %while.26 = (s32[]{:T(128)}, bf16[2,512,8,64]{1,3,2,0:T(8,128)(2,1)}, f32[2,8,512]{2,1,0:T(8,128)S(1)}, bf16[2,512,8,64]{1,3,2,0:T(8,128)(2,1)S(1)}, bf16[2,512,...) while((s32[]{:T(128)}, bf16[2,512,8,64]{1,3,2,0:T(8,128)(2,1)}, ...), condition=%wide.region_3.5_spmd, body=%wide.region_0.4_spmd.sunk | while | flops 553906176 | bytes 35784840 | solution.py:139
  68.5 1.6 fusion.152
  73.8 1.6 fusion.152
  76.3 3.2 copy.61
  80.8 3.3 fusion.94
  84.8 12.7 %reduce-scatter.5.cloned.1.call-done = f32[512,1024]{1,0:T(8,128)} async-done(((f32[1024,1024]{1,0:T(8,128)}), f32[512,1024]{1,0:T(8,128)}) %reduce-scatter.5.cloned.1.call-update) | async-done | bytes 2097168 | tf_op jit(solution)/shard_map/reduce_scatter | solution.py:141
  97.5 2.5 fusion.91
  101.9 12.0 %all-gather.7.cloned.1.call-done = bf16[1024,1024]{1,0:T(8,128)(2,1)} async-done(((bf16[512,1024]{1,0:T(8,128)(2,1)}), bf16[1024,1024]{1,0:T(8,128)(2,1)}) %all-gather.7.cloned.1.call-update) | async-done | bytes 2097168 | tf_op jit(solution)/shard_map/all_gather | solution.py:152
  113.8 25.3 %fusion.60 = (bf16[1024,2048]{1,0:T(8,128)(2,1)S(1)}, f32[1024,2048]{1,0:T(8,128)}) fusion(f32[2048]{0:T(1024)S(1)} %convert_element_type.185, bf16[1024,1024]{1,0:T(8,128)(2,1)} %all-gather.7.cloned.1.call-done, bf16[1024,2048]{1,0:T(8,128)(2,1)} %param.41), kind=kOutput, calls=%fused_computation.71 | convolution fusion | flops 4433379328 | bytes 18882560 | tf_op jit(solution)/shard_map/dot_general | solution.py:153
  139.1 2.0 copy-done.61
  141.1 6.0 fusion.95
  147.8 12.7 %reduce-scatter.7.cloned.1.call-done = f32[512,1024]{1,0:T(8,128)} async-done(((f32[1024,1024]{1,0:T(8,128)}), f32[512,1024]{1,0:T(8,128)}) %reduce-scatter.7.cloned.1.call-update) | async-done | bytes 2097168 | tf_op jit(solution)/shard_map/reduce_scatter | solution.py:155
  160.5 2.3 fusion.90
  164.8 2.4 fusion.87
  169.9 11.8 %all-gather.9.cloned.1.call-done = bf16[1024,1024]{1,0:T(8,128)(2,1)} async-done(((bf16[512,1024]{1,0:T(8,128)(2,1)}), bf16[1024,1024]{1,0:T(8,128)(2,1)}) %all-gather.9.cloned.1.call-update) | async-done | bytes 2097168 | tf_op jit(solution)/shard_map/all_gather | solution.py:172
  181.7 11.5 %fusion.93 = (bf16[2048]{0:T(1024)(128)(2,1)}, bf16[1024,2048]{1,0:T(8,128)(2,1)S(1)}) fusion(f32[1024,2048]{1,0:T(8,128)} %get-tuple-element.213, f32[2048]{0:T(1024)S(1)} %convert_element_type.185, bf16[1024,1024]{1,0:T(8,128)(2,1)} %all-gather.9.cloned.1.call-done, bf16[2048,1024]{1,0:T(8,128)(2,1)} %param.43), kind=kOutput, calls=%fused_computation.173 | convolution fusion | flops 4320131072 | bytes 18886656 | tf_op jit(solution)/shard_map/dot_general | solution.py:18
  193.2 2.0 copy-done.59
  195.2 6.1 fusion.96
  201.3 13.3 %reduce-scatter.9.cloned.1.call-done = f32[512,1024]{1,0:T(8,128)} async-done(((f32[1024,1024]{1,0:T(8,128)}), f32[512,1024]{1,0:T(8,128)}) %reduce-scatter.9.cloned.1.call-update) | async-done | bytes 2097168 | tf_op jit(solution)/shard_map/reduce_scatter | solution.py:177
  214.6 3.2 multiply_reduce_fusion.2
  221.2 11.8 %all-gather.11.cloned.1.call-done = bf16[1024,1024]{1,0:T(8,128)(2,1)} async-done(((bf16[512,1024]{1,0:T(8,128)(2,1)}), bf16[1024,1024]{1,0:T(8,128)(2,1)}) %all-gather.11.cloned.1.call-update) | async-done | bytes 2097168 | tf_op jit(solution)/shard_map/all_gather | solution.py:183
  233.0 3.8 convolution_convert_fusion.6
  236.9 4.0 reshape.217
  240.9 3.3 copy.65
  247.4 23.9 %while.27 = (s32[]{:T(128)}, bf16[2,512,8,64]{1,3,2,0:T(8,128)(2,1)}, bf16[2,512,8,64]{1,3,2,0:T(8,128)(2,1)}, bf16[2,512,8,64]{1,3,2,0:T(8,128)(2,1)}, bf16[2,5...) while((s32[]{:T(128)}, ...), condition=%wide.region_17.19_spmd, body=%wide.region_15.18_spmd.sunk | while | flops 1368649728 | bytes 89249008 | solution.py:186
  248.8 2.3 multiply_reduce_fusion.10
  251.1 2.6 multiply_convert_fusion.2
  256.9 2.4 fusion.164
  260.6 2.3 multiply_reduce_fusion.10
  262.9 2.6 multiply_convert_fusion.2
  268.7 2.4 fusion.164
  271.4 2.5 copy.69
  279.7 2.7 add_convert_fusion
  283.0 9.5 %convolution_convert_fusion = bf16[2048,1024]{1,0:T(8,128)(2,1)} fusion(bf16[1024,2048]{1,0:T(8,128)(2,1)} %copy-done.61, bf16[1024,1024]{1,0:T(8,128)(2,1)} %all-gather.9.cloned.1.call-done), kind=kOutput, calls=%fused_computation.94 | convolution fusion | flops 4297064448 | bytes 10485760 | tf_op jit(solution)/shard_map/dot_general | solution.py:12
  292.5 6.2 convolution_convert_fusion.1
  298.8 2.3 convolution_convert_fusion.2
  301.1 2.3 convolution_convert_fusion.3
  303.4 2.3 convolution_convert_fusion.4
  305.7 2.3 convolution_convert_fusion.5
  308.7 44.8 %all-reduce = (f32[1024]{0:T(1024)}, f32[1024]{0:T(1024)}, f32[1024]{0:T(1024)}, f32[1024]{0:T(1024)}, f32[1024]{0:T(1024)}, /*index=5*/f32[1024]{0:T(1024)}) all-reduce(f32[1024]{0:T(1024)S(1)} %get-tuple-element.196, f32[1024]{0:T(1024)S(1)} %get-tuple-element.135, ...), channel_id=1, replica_groups=mesh['batch'=16,'mp'=2] {'batch','mp'}, use_global_device_ids=true, to_apply=%region_28.30 | all-reduce | flops 6144 | bytes 49152 | tf_op jit(solution)/shard_map/psum | solution.py:226
  355.3 44.0 %all-reduce.1 = (bf16[512]{0:T(512)(128)(2,1)S(1)}, bf16[512]{0:T(512)(128)(2,1)S(1)}, bf16[2048]{0:T(1024)(128)(2,1)S(1)}) all-reduce(bf16[512]{0:T(512)(128)(2,1)S(1)} %reduce_sum.193, bf16[512]{0:T(512)(128)(2,1)S(1)} %reduce_sum.195, bf16[2048]{0:T(1024)(128)(2,1)S(1)} %copy-done.43), channel_id=1, replica_groups=mesh['batch'=16,'mp'=2] {'batch'}, use_global_device_ids=true, to_apply=%region_21.23 | all-reduce | flops 3072 | bytes 12288 | tf_op jit(solution)/shard_map/psum | solution.py:217
  401.1 3.0 convert_add_fusion
  404.0 271.6 %all-reduce.5.cloned.1.call-done = (bf16[1024,512]{1,0:T(8,128)(2,1)}, bf16[1024,512]{1,0:T(8,128)(2,1)}, bf16[1024,512]{1,0:T(8,128)(2,1)}, bf16[512,1024]{1,0:...) async-done(((bf16[1024,512]{1,0:T(8,128)(2,1)}, bf16[1024,512]{1,0:T(8,128)(2,1)}, bf16[1024,512]{1,0:T(8,128)(2,1)}, bf16[512,1024]{1,0:T(8,128)(2,1)}, ...) | async-done | bytes 12582928 | tf_op jit(solution)/shard_map/psum | solution.py:216
  675.7 6.8 convert_element_type.209
  682.5 4.4 convert_element_type.212
  686.9 1.6 convert_element_type.199
  688.6 1.6 convert_element_type.202
  690.2 1.6 convert_element_type.204
  691.8 1.6 convert_element_type.207
  (228 shorter events, 47.4 us)
Async XLA Ops:
  7.2 3.7 copy-start
  7.2 34.3 %all-gather.5.cloned.1.call-start = ((), (), s32[]{:S(2)}) async-start(), calls=%async_computation.4 | async-start | bytes 3145728 | tf_op jit(solution)/shard_map/all_gather | solution.py:125
  15.7 5.5 copy-start.2
  24.0 4.2 copy-start.50
  24.0 4.2 copy-start.51
  24.0 17.5 %copy-start.25 = (bf16[1024,512]{1,0:T(8,128)(2,1)S(1)}, bf16[1024,512]{1,0:T(8,128)(2,1)}, u32[]{:S(2)}) copy-start(bf16[1024,512]{1,0:T(8,128)(2,1)} %param.35) | copy-start | bytes 3145732
  28.1 69.4 %reduce-scatter.5.cloned.1.call-start = ((), (), s32[]{:S(2)}) async-start(), calls=%async_computation.5 | async-start | bytes 6291456 | tf_op jit(solution)/shard_map/reduce_scatter | solution.py:141
  67.0 1.4 copy-start.22
  72.3 1.4 copy-start.22
  76.3 7.8 %copy-start.3 = (bf16[2,512,8,64]{1,3,2,0:T(8,128)(2,1)}, bf16[2,512,8,64]{1,3,2,0:T(8,128)(2,1)S(1)}, u32[]{:S(2)}) copy-start(bf16[2,512,8,64]{1,3,2,0:T(8,128)(2,1)S(1)} %get-tuple-element.399) | copy-start | bytes 3145732
  76.3 7.8 %copy-start.5 = (bf16[2,512,8,64]{1,3,2,0:T(8,128)(2,1)}, bf16[2,512,8,64]{1,3,2,0:T(8,128)(2,1)S(1)}, u32[]{:S(2)}) copy-start(bf16[2,512,8,64]{1,3,2,0:T(8,128)(2,1)S(1)} %get-tuple-element.400) | copy-start | bytes 3145732
  76.3 7.8 %copy-start.7 = (bf16[2,512,8,64]{1,3,2,0:T(8,128)(2,1)}, bf16[2,512,8,64]{1,3,2,0:T(8,128)(2,1)S(1)}, u32[]{:S(2)}) copy-start(bf16[2,512,8,64]{1,3,2,0:T(8,128)(2,1)S(1)} %get-tuple-element.401) | copy-start | bytes 3145732
  76.3 7.8 %copy-start.37 = (f32[2,8,512]{2,1,0:T(8,128)}, f32[2,8,512]{2,1,0:T(8,128)S(1)}, u32[]{:S(2)}) copy-start(f32[2,8,512]{2,1,0:T(8,128)S(1)} %get-tuple-element.355) | copy-start | bytes 98308
  76.3 4.4 copy-start.35
  80.8 3.9 copy-start.44
  80.8 4.0 copy-start.45
  80.8 4.0 copy-start.46
  84.1 29.7 %all-gather.7.cloned.1.call-start = ((), (), s32[]{:S(2)}) async-start(), calls=%async_computation.6 | async-start | bytes 3145728 | tf_op jit(solution)/shard_map/all_gather | solution.py:152
  100.0 1.8 copy-start.42
  101.8 58.7 %reduce-scatter.7.cloned.1.call-start = ((), (), s32[]{:S(2)}) async-start(), calls=%async_computation.7 | async-start | bytes 6291456 | tf_op jit(solution)/shard_map/reduce_scatter | solution.py:155
  113.8 27.3 %copy-start.52 = (bf16[2048,1024]{1,0:T(8,128)(2,1)S(1)}, bf16[2048,1024]{1,0:T(8,128)(2,1)}, u32[]{:S(2)}) copy-start(bf16[2048,1024]{1,0:T(8,128)(2,1)} %param.43) | copy-start | bytes 12582916
  139.1 2.0 copy-start.61
  147.1 34.6 %all-gather.9.cloned.1.call-start = ((), (), s32[]{:S(2)}) async-start(), calls=%async_computation.8 | async-start | bytes 3145728 | tf_op jit(solution)/shard_map/all_gather | solution.py:172
  147.8 15.4 %copy-start.24 = (bf16[512,1024]{1,0:T(8,128)(2,1)S(1)}, bf16[512,1024]{1,0:T(8,128)(2,1)}, u32[]{:S(2)}) copy-start(bf16[512,1024]{1,0:T(8,128)(2,1)} %param.47) | copy-start | bytes 3145732
  169.7 45.0 %reduce-scatter.9.cloned.1.call-start = ((), (), s32[]{:S(2)}) async-start(), calls=%async_computation.9 | async-start | bytes 6291456 | tf_op jit(solution)/shard_map/reduce_scatter | solution.py:177
  181.7 13.5 %copy-start.53 = (bf16[1024,2048]{1,0:T(8,128)(2,1)S(1)}, bf16[1024,2048]{1,0:T(8,128)(2,1)}, u32[]{:S(2)}) copy-start(bf16[1024,2048]{1,0:T(8,128)(2,1)} %param.41) | copy-start | bytes 12582916
  193.2 2.0 copy-start.59
  201.3 31.7 %all-gather.11.cloned.1.call-start = ((), (), s32[]{:S(2)}) async-start(), calls=%async_computation.10 | async-start | bytes 3145728 | tf_op jit(solution)/shard_map/all_gather | solution.py:183
  217.8 15.2 %copy-start.36 = (bf16[512,1024]{1,0:T(8,128)(2,1)S(1)}, bf16[512,1024]{1,0:T(8,128)(2,1)}, u32[]{:S(2)}) copy-start(bf16[512,1024]{1,0:T(8,128)(2,1)} %param.37) | copy-start | bytes 3145732
  221.0 180.1 %reduce-scatter.11.cloned.1.call-start = ((), (), s32[]{:S(2)}) async-start(), calls=%async_computation.11 | async-start | bytes 3145728 | tf_op jit(solution)/shard_map/reduce_scatter | solution.py:195
  236.8 10.6 %copy-start.4 = (bf16[2,512,8,64]{1,3,2,0:T(8,128)(2,1)S(1)}, bf16[2,512,8,64]{1,3,2,0:T(8,128)(2,1)}, u32[]{:S(2)}) copy-start(bf16[2,512,8,64]{1,3,2,0:T(8,128)(2,1)} %copy-done.3) | copy-start | bytes 3145732
  236.8 10.6 %copy-start.6 = (bf16[2,512,8,64]{1,3,2,0:T(8,128)(2,1)S(1)}, bf16[2,512,8,64]{1,3,2,0:T(8,128)(2,1)}, u32[]{:S(2)}) copy-start(bf16[2,512,8,64]{1,3,2,0:T(8,128)(2,1)} %copy-done.5) | copy-start | bytes 3145732
  236.8 10.6 %copy-start.8 = (bf16[2,512,8,64]{1,3,2,0:T(8,128)(2,1)S(1)}, bf16[2,512,8,64]{1,3,2,0:T(8,128)(2,1)}, u32[]{:S(2)}) copy-start(bf16[2,512,8,64]{1,3,2,0:T(8,128)(2,1)} %copy-done.7) | copy-start | bytes 3145732
  236.8 10.6 %copy-start.38 = (f32[2,8,512]{2,1,0:T(8,128)S(1)}, f32[2,8,512]{2,1,0:T(8,128)}, u32[]{:S(2)}) copy-start(f32[2,8,512]{2,1,0:T(8,128)} %copy-done.37) | copy-start | bytes 98308
  247.4 1.3 copy-start.9
  251.1 2.6 copy-start.19
  253.7 1.4 copy-start.13
  255.1 1.8 copy-start.20
  259.3 1.3 copy-start.9
  262.9 2.6 copy-start.19
  265.5 1.4 copy-start.13
  266.9 1.8 copy-start.20
  271.3 2.7 copy-start.21
  271.3 4.1 copy-start.15
  274.1 2.7 copy-start.57
  275.4 2.7 copy-start.31
  276.8 1.4 copy-start.33
  276.8 1.6 copy-start.58
  282.4 393.2 %all-reduce.5.cloned.1.call-start = ((), (), s32[]{:S(2)}) async-start(), calls=%async_computation.12 | async-start | bytes 25165824 | tf_op jit(solution)/shard_map/psum | solution.py:216
  282.9 9.5 %copy-start.55 = (bf16[1024,1024]{1,0:T(8,128)(2,1)S(1)}, bf16[1024,1024]{1,0:T(8,128)(2,1)}, u32[]{:S(2)}) copy-start(bf16[1024,1024]{1,0:T(8,128)(2,1)} %all-gather.7.cloned.1.call-done) | copy-start | bytes 6291460
  283.0 9.5 %copy-start.60 = (bf16[1024,2048]{1,0:T(8,128)(2,1)S(1)}, bf16[1024,2048]{1,0:T(8,128)(2,1)}, u32[]{:S(2)}) copy-start(bf16[1024,2048]{1,0:T(8,128)(2,1)} %copy-done.59) | copy-start | bytes 12582916
  292.5 6.3 copy-start.17
  292.5 6.3 copy-start.56
  298.8 2.3 copy-start.54
  301.1 2.3 copy-start.32
  303.4 2.3 copy-start.34
  307.9 47.3 %copy-start.43 = (bf16[2048]{0:T(1024)(128)(2,1)S(1)}, bf16[2048]{0:T(1024)(128)(2,1)}, u32[]{:S(2)}) copy-start(bf16[2048]{0:T(1024)(128)(2,1)} %get-tuple-element.214) | copy-start | bytes 12292
  307.9 93.1 %copy-start.11 = (f32[512,1024]{1,0:T(8,128)S(1)}, f32[512,1024]{1,0:T(8,128)}, u32[]{:S(2)}) copy-start(f32[512,1024]{1,0:T(8,128)} %copy-done.10) | copy-start | bytes 6291460
  675.7 6.8 copy-start.18
  682.5 4.4 copy-start.30
  682.5 6.1 copy-start.29
  686.9 3.2 copy-start.28
  686.9 4.8 copy-start.27
  688.5 4.8 copy-start.1
  (14 other events, 13.0 us)
Sparse Core Ops, SparseCore 0:
  28.2 13.2 all-gather.4
  84.3 13.1 reduce-scatter.4
  101.9 11.8 all-gather.6
  147.2 13.2 reduce-scatter.6
  169.8 11.8 all-gather.8
  201.4 13.2 reduce-scatter.8
  221.1 11.8 all-gather.10
  282.6 10.7 reduce-scatter.10
  308.1 367.5 all-reduce.4
where the time goes:
time: 706 us; the launch traced here: 700 us
  waiting for transfers between devices  359 us (51%)
  matrix products  117 us (17%)
  blocking collectives  88.8 us (13%)
  local copies, waits for them, and re-layouts  64.2 us (9%)
  other arithmetic  53.5 us (8%)
  between operations  14.7 us (2%)
    psum x1, waiting for transfers between devices, shards(): lax.psum(grad_w_query.astype(jnp.bfloat16), 'batch').astype(jnp.float32)  272 us
    psum x1, blocking collectives, shards(): lax.psum((grad_b_out, grad_ln1_gain, grad_ln1_bias, grad_b_down, grad_ln2...  44.8 us
    psum x1, blocking collectives, shards(): lax.psum(grad_b_query.astype(jnp.bfloat16), 'batch').astype(jnp.float32)  44 us
    dot_general x6, matrix products, contract_last(): lax.dot_general(left, right, (((1,), (1,)), ((), ())), preferred_element_...  26.7 us
    dot_general x1, matrix products, shards(): jnp.dot(mid_all, w_up, preferred_element_type=jnp.float32)  25.3 us
    dot_general x6, matrix products, contract_rows(): lax.dot_general(left, right, (((0,), (0,)), ((), ())), preferred_element_...  24.9 us
  transfers between devices with their start and end apart: 9, of which 8 were waited for; matrix products, arithmetic and copies ran while one was open for 5% of the time, Pallas kernels for 0%

commit v1 on v0

--- a/solution.py
+++ b/solution.py
@@ -213,7 +213,9 @@
         grad_b_up,
         grad_w_down,
     ) = (
-        lax.psum(grad_w_query.astype(jnp.bfloat16), "batch").astype(jnp.float32),
+        jnp.sum(lax.all_gather(grad_w_query.astype(jnp.bfloat16), "batch"), axis=0).astype(
+            jnp.float32
+        ),
         lax.psum(grad_b_query.astype(jnp.bfloat16), "batch").astype(jnp.float32),
         lax.psum(grad_w_key.astype(jnp.bfloat16), "batch").astype(jnp.float32),
         lax.psum(grad_w_value.astype(jnp.bfloat16), "batch").astype(jnp.float32),

time: 706 us -> 864 us (1.22)
  waiting for transfers between devices: 359 us -> 507 us
  other arithmetic: 53.5 us -> 63.1 us
    all_gather x0 -> x1, waiting for transfers between devices: none -> 176 us  [shards(): lax.all_gather(grad_w_query.astype(jnp.bfloat16), 'batch')]
    psum x1, waiting for transfers between devices: 272 us -> 243 us  [shards(): lax.psum(grad_w_key.astype(jnp.bfloat16), 'batch').astype(jnp.float32)]
    reduce_sum x0 -> x1, other arithmetic: none -> 9.04 us  [shards(): jnp.sum(lax.all_gather(grad_w_query.astype(jnp.bfloat16), 'batch'), axis=0)]
  transfers between devices with their start and end apart: 9 -> 10, of which waited for: 8 -> 9; matrix products, arithmetic and copies ran while one was open for 5% -> 6% of each run, Pallas kernels for 0% -> 0%
where the time goes in v1:
time: 864 us; the launch traced here: 858 us
  waiting for transfers between devices  507 us (59%)
  matrix products  118 us (14%)
  blocking collectives  89.4 us (10%)
  local copies, waits for them, and re-layouts  64.3 us (7%)
  other arithmetic  63.1 us (7%)
  between operations  15.1 us (2%)
    psum x1, waiting for transfers between devices, shards(): lax.psum(grad_w_key.astype(jnp.bfloat16), 'batch').astype(jnp.float32)  243 us
    all_gather x1, waiting for transfers between devices, shards(): lax.all_gather(grad_w_query.astype(jnp.bfloat16), 'batch')  176 us
    psum x1, blocking collectives, shards(): lax.psum(grad_b_query.astype(jnp.bfloat16), 'batch').astype(jnp.float32)  45.1 us
    psum x1, blocking collectives, shards(): lax.psum((grad_b_out, grad_ln1_gain, grad_ln1_bias, grad_b_down, grad_ln2...  44.3 us
    dot_general x6, matrix products, contract_rows(): lax.dot_general(left, right, (((0,), (0,)), ((), ())), preferred_element_...  26.9 us
    dot_general x6, matrix products, contract_last(): lax.dot_general(left, right, (((1,), (1,)), ((), ())), preferred_element_...  26.7 us
    dot_general x1, matrix products, shards(): jnp.dot(mid_all, w_up, preferred_element_type=jnp.float32)  25.3 us
  transfers between devices with their start and end apart: 10, of which 9 were waited for; matrix products, arithmetic and copies ran while one was open for 6% of the time, Pallas kernels for 0%

profile of v1, /device:TPU:0, one launch (start us, length us, event | category | flops | bytes accessed | tf_op | source)
XLA Modules:
  0.0 858.5 jit_solution(6982019583735948537)
XLA Ops:
  10.9 2.1 gather_fusion.1
  13.0 2.8 gather_fusion.3
  15.7 5.5 gather_fusion.2
  21.2 2.8 gather_fusion.4
  24.0 4.1 fusion.92
  28.2 13.3 %all-gather.7.cloned.1.call-done = bf16[1024,1024]{1,0:T(8,128)(2,1)} async-done(((bf16[512,1024]{1,0:T(8,128)(2,1)}), bf16[1024,1024]{1,0:T(8,128)(2,1)}) %all-gather.7.cloned.1.call-update) | async-done | bytes 2097168 | tf_op jit(solution)/shard_map/all_gather | solution.py:125
  41.5 2.8 add_convert_fusion.3
  44.4 2.4 reshape.219
  46.7 2.5 copy.58
  49.2 3.1 add_convert_fusion.2
  52.3 2.1 reshape.220
  54.4 2.5 copy.59
  56.9 3.1 convolution_convert_fusion.7
  60.0 2.1 reshape.221
  62.1 2.5 copy.60
  65.7 10.6 %while.26 = (s32[]{:T(128)}, bf16[2,512,8,64]{1,3,2,0:T(8,128)(2,1)}, f32[2,8,512]{2,1,0:T(8,128)S(1)}, bf16[2,512,8,64]{1,3,2,0:T(8,128)(2,1)S(1)}, bf16[2,512,...) while((s32[]{:T(128)}, bf16[2,512,8,64]{1,3,2,0:T(8,128)(2,1)}, ...), condition=%wide.region_3.5_spmd, body=%wide.region_0.4_spmd.sunk | while | flops 553906176 | bytes 35784848 | solution.py:139
  68.5 1.6 fusion.152
  73.8 1.6 fusion.152
  76.3 3.2 copy.61
  80.8 3.3 fusion.94
  84.8 12.7 %reduce-scatter.5.cloned.1.call-done = f32[512,1024]{1,0:T(8,128)} async-done(((f32[1024,1024]{1,0:T(8,128)}), f32[512,1024]{1,0:T(8,128)}) %reduce-scatter.5.cloned.1.call-update) | async-done | bytes 2097168 | tf_op jit(solution)/shard_map/reduce_scatter | solution.py:141
  97.5 2.5 fusion.91
  101.9 11.9 %all-gather.9.cloned.1.call-done = bf16[1024,1024]{1,0:T(8,128)(2,1)} async-done(((bf16[512,1024]{1,0:T(8,128)(2,1)}), bf16[1024,1024]{1,0:T(8,128)(2,1)}) %all-gather.9.cloned.1.call-update) | async-done | bytes 2097168 | tf_op jit(solution)/shard_map/all_gather | solution.py:152
  113.9 25.3 %fusion.60 = (bf16[1024,2048]{1,0:T(8,128)(2,1)S(1)}, f32[1024,2048]{1,0:T(8,128)}) fusion(f32[2048]{0:T(1024)S(1)} %convert_element_type.187, bf16[1024,1024]{1,0:T(8,128)(2,1)} %all-gather.9.cloned.1.call-done, bf16[1024,2048]{1,0:T(8,128)(2,1)} %param.41), kind=kOutput, calls=%fused_computation.71 | convolution fusion | flops 4433379328 | bytes 18882560 | tf_op jit(solution)/shard_map/dot_general | solution.py:153
  139.2 2.0 copy-done.60
  141.1 6.0 fusion.95
  147.8 12.7 %reduce-scatter.7.cloned.1.call-done = f32[512,1024]{1,0:T(8,128)} async-done(((f32[1024,1024]{1,0:T(8,128)}), f32[512,1024]{1,0:T(8,128)}) %reduce-scatter.7.cloned.1.call-update) | async-done | bytes 2097168 | tf_op jit(solution)/shard_map/reduce_scatter | solution.py:155
  160.5 2.3 fusion.90
  164.8 2.4 fusion.87
  169.9 11.8 %all-gather.11.cloned.1.call-done = bf16[1024,1024]{1,0:T(8,128)(2,1)} async-done(((bf16[512,1024]{1,0:T(8,128)(2,1)}), bf16[1024,1024]{1,0:T(8,128)(2,1)}) %all-gather.11.cloned.1.call-update) | async-done | bytes 2097168 | tf_op jit(solution)/shard_map/all_gather | solution.py:172
  181.7 11.5 %fusion.93 = (bf16[2048]{0:T(1024)(128)(2,1)}, bf16[1024,2048]{1,0:T(8,128)(2,1)S(1)}) fusion(f32[1024,2048]{1,0:T(8,128)} %get-tuple-element.212, f32[2048]{0:T(1024)S(1)} %convert_element_type.187, bf16[1024,1024]{1,0:T(8,128)(2,1)} %all-gather.11.cloned.1.call-done, bf16[2048,1024]{1,0:T(8,128)(2,1)} %param.43), kind=kOutput, calls=%fused_computation.173 | convolution fusion | flops 4320131072 | bytes 18886656 | tf_op jit(solution)/shard_map/dot_general | solution.py:18
  193.2 2.0 copy-done.58
  195.2 6.1 fusion.96
  201.3 13.3 %reduce-scatter.9.cloned.1.call-done = f32[512,1024]{1,0:T(8,128)} async-done(((f32[1024,1024]{1,0:T(8,128)}), f32[512,1024]{1,0:T(8,128)}) %reduce-scatter.9.cloned.1.call-update) | async-done | bytes 2097168 | tf_op jit(solution)/shard_map/reduce_scatter | solution.py:177
  214.6 3.2 multiply_reduce_fusion.2
  221.2 11.8 %all-gather.13.cloned.1.call-done = bf16[1024,1024]{1,0:T(8,128)(2,1)} async-done(((bf16[512,1024]{1,0:T(8,128)(2,1)}), bf16[1024,1024]{1,0:T(8,128)(2,1)}) %all-gather.13.cloned.1.call-update) | async-done | bytes 2097168 | tf_op jit(solution)/shard_map/all_gather | solution.py:183
  233.0 3.8 convolution_convert_fusion.6
  236.9 4.0 reshape.218
  240.9 3.3 copy.65
  247.4 23.0 %while.27 = (s32[]{:T(128)}, bf16[2,512,8,64]{1,3,2,0:T(8,128)(2,1)}, bf16[2,512,8,64]{1,3,2,0:T(8,128)(2,1)}, bf16[2,512,8,64]{1,3,2,0:T(8,128)(2,1)}, bf16[2,5...) while((s32[]{:T(128)}, ...), condition=%wide.region_17.19_spmd, body=%wide.region_15.18_spmd.sunk | while | flops 1368649728 | bytes 97637696 | solution.py:186
  250.6 2.3 multiply_reduce_fusion.10
  252.9 2.6 multiply_convert_fusion.2
  262.0 2.3 multiply_reduce_fusion.10
  264.3 2.6 multiply_convert_fusion.2
  270.5 2.5 copy.68
  278.9 2.7 add_convert_fusion
  282.1 9.5 %convolution_convert_fusion = bf16[2048,1024]{1,0:T(8,128)(2,1)} fusion(bf16[1024,2048]{1,0:T(8,128)(2,1)} %copy-done.60, bf16[1024,1024]{1,0:T(8,128)(2,1)} %all-gather.11.cloned.1.call-done), kind=kOutput, calls=%fused_computation.94 | convolution fusion | flops 4297064448 | bytes 10485760 | tf_op jit(solution)/shard_map/dot_general | solution.py:12
  291.7 6.2 convolution_convert_fusion.1
  297.9 2.3 convolution_convert_fusion.2
  300.2 2.3 convolution_convert_fusion.3
  302.5 2.3 convolution_convert_fusion.4
  304.9 4.3 convolution_convert_fusion.5
  309.2 44.3 %all-reduce = (f32[1024]{0:T(1024)}, f32[1024]{0:T(1024)}, f32[1024]{0:T(1024)}, f32[1024]{0:T(1024)}, f32[1024]{0:T(1024)}, /*index=5*/f32[1024]{0:T(1024)}) all-reduce(f32[1024]{0:T(1024)S(1)} %get-tuple-element.195, f32[1024]{0:T(1024)S(1)} %get-tuple-element.135, ...), channel_id=1, replica_groups=mesh['batch'=16,'mp'=2] {'batch','mp'}, use_global_device_ids=true, to_apply=%region_28.30 | all-reduce | flops 6144 | bytes 49152 | tf_op jit(solution)/shard_map/psum | solution.py:228
  355.4 45.1 %all-reduce.1 = (bf16[512]{0:T(512)(128)(2,1)S(1)}, bf16[512]{0:T(512)(128)(2,1)S(1)}, bf16[2048]{0:T(1024)(128)(2,1)S(1)}) all-reduce(bf16[512]{0:T(512)(128)(2,1)S(1)} %reduce_sum.206, bf16[512]{0:T(512)(128)(2,1)S(1)} %reduce_sum.208, bf16[2048]{0:T(1024)(128)(2,1)S(1)} %copy-done.42), channel_id=1, replica_groups=mesh['batch'=16,'mp'=2] {'batch'}, use_global_device_ids=true, to_apply=%region_21.23 | all-reduce | flops 3072 | bytes 12288 | tf_op jit(solution)/shard_map/psum | solution.py:219
  402.3 3.0 convert_add_fusion
  405.3 242.7 %all-reduce.5.cloned.1.call-done = (bf16[1024,512]{1,0:T(8,128)(2,1)}, bf16[1024,512]{1,0:T(8,128)(2,1)}, bf16[512,1024]{1,0:T(8,128)(2,1)}, bf16[1024,2048]{1,0:T(8,128)(2,1)}, bf16[2048,1024]{1,0:T(8,128)(2,1)}) async-done(((bf16[1024,512]{1,0:T(8,128)(2,1)}, bf16[1024,512]{1,0:T(8,128)(2,1)}, bf16[512,1024]{1,0:T(8,128)(2,1)}, bf16[1024,2048]{1,0:T(8,128)(2,1)}, bf16[2048,1024]{1,0:T(8,128)(2,1)}), ...) | async-done | bytes 11534352 | tf_op jit(solution)/shard_map/psum | solution.py:220
  648.0 3.0 convert_element_type.204
  651.0 2.8 convert_element_type.206
  653.8 1.6 convert_element_type.209
  655.4 4.8 convert_element_type.211
  660.2 4.4 convert_element_type.214
  664.7 176.1 %all-gather.15.cloned.1.call-done = bf16[16384,512]{1,0:T(8,128)(2,1)} async-done(((bf16[1024,512]{1,0:T(8,128)(2,1)}), bf16[16384,512]{1,0:T(8,128)(2,1)}) %all-gather.15.cloned.1.call-update) | async-done | bytes 16777232 | tf_op jit(solution)/shard_map/all_gather | solution.py:216
  840.8 9.0 %reduce_sum.204 = bf16[1024,512]{1,0:T(8,128)(2,1)S(1)} reduce(bf16[16,1024,512]{2,1,0:T(8,128)(2,1)} %bitcast.162, bf16[]{:T(256)} %constant.89.clone.1), dimensions={0}, to_apply=%region_19.21 | reduce | flops 7864320 | bytes 17825794 | tf_op jit(solution)/shard_map/reduce_sum | solution.py:216
  849.8 1.6 convert_element_type.201
  (234 shorter events, 50.7 us)
Async XLA Ops:
  7.2 3.7 copy-start
  7.2 34.3 %all-gather.7.cloned.1.call-start = ((), (), s32[]{:S(2)}) async-start(), calls=%async_computation.4 | async-start | bytes 3145728 | tf_op jit(solution)/shard_map/all_gather | solution.py:125
  15.7 5.5 copy-start.2
  24.0 4.2 copy-start.49
  24.0 4.2 copy-start.50
  24.0 17.5 %copy-start.28 = (bf16[1024,512]{1,0:T(8,128)(2,1)S(1)}, bf16[1024,512]{1,0:T(8,128)(2,1)}, u32[]{:S(2)}) copy-start(bf16[1024,512]{1,0:T(8,128)(2,1)} %param.35) | copy-start | bytes 3145732
  28.1 69.5 %reduce-scatter.5.cloned.1.call-start = ((), (), s32[]{:S(2)}) async-start(), calls=%async_computation.5 | async-start | bytes 6291456 | tf_op jit(solution)/shard_map/reduce_scatter | solution.py:141
  67.0 1.4 copy-start.25
  72.3 1.4 copy-start.25
  76.3 7.8 copy-start.3
  76.3 7.8 copy-start.5
  76.3 7.8 copy-start.7
  76.3 7.8 copy-start.36
  76.3 4.5 copy-start.34
  80.8 3.9 copy-start.43
  80.8 4.0 copy-start.44
  80.8 4.0 copy-start.45
  84.2 29.7 %all-gather.9.cloned.1.call-start = ((), (), s32[]{:S(2)}) async-start(), calls=%async_computation.6 | async-start | bytes 3145728 | tf_op jit(solution)/shard_map/all_gather | solution.py:152
  100.1 1.8 copy-start.41
  101.9 58.7 %reduce-scatter.7.cloned.1.call-start = ((), (), s32[]{:S(2)}) async-start(), calls=%async_computation.7 | async-start | bytes 6291456 | tf_op jit(solution)/shard_map/reduce_scatter | solution.py:155
  113.9 27.2 %copy-start.51 = (bf16[2048,1024]{1,0:T(8,128)(2,1)S(1)}, bf16[2048,1024]{1,0:T(8,128)(2,1)}, u32[]{:S(2)}) copy-start(bf16[2048,1024]{1,0:T(8,128)(2,1)} %param.43) | copy-start | bytes 12582916
  139.2 2.0 copy-start.60
  147.2 34.6 %all-gather.11.cloned.1.call-start = ((), (), s32[]{:S(2)}) async-start(), calls=%async_computation.8 | async-start | bytes 3145728 | tf_op jit(solution)/shard_map/all_gather | solution.py:172
  147.8 15.4 %copy-start.27 = (bf16[512,1024]{1,0:T(8,128)(2,1)S(1)}, bf16[512,1024]{1,0:T(8,128)(2,1)}, u32[]{:S(2)}) copy-start(bf16[512,1024]{1,0:T(8,128)(2,1)} %param.47) | copy-start | bytes 3145732
  169.7 44.9 %reduce-scatter.9.cloned.1.call-start = ((), (), s32[]{:S(2)}) async-start(), calls=%async_computation.9 | async-start | bytes 6291456 | tf_op jit(solution)/shard_map/reduce_scatter | solution.py:177
  181.7 13.5 %copy-start.52 = (bf16[1024,2048]{1,0:T(8,128)(2,1)S(1)}, bf16[1024,2048]{1,0:T(8,128)(2,1)}, u32[]{:S(2)}) copy-start(bf16[1024,2048]{1,0:T(8,128)(2,1)} %param.41) | copy-start | bytes 12582916
  193.2 2.0 copy-start.58
  201.3 31.7 %all-gather.13.cloned.1.call-start = ((), (), s32[]{:S(2)}) async-start(), calls=%async_computation.10 | async-start | bytes 3145728 | tf_op jit(solution)/shard_map/all_gather | solution.py:183
  217.8 15.2 %copy-start.35 = (bf16[512,1024]{1,0:T(8,128)(2,1)S(1)}, bf16[512,1024]{1,0:T(8,128)(2,1)}, u32[]{:S(2)}) copy-start(bf16[512,1024]{1,0:T(8,128)(2,1)} %param.37) | copy-start | bytes 3145732
  221.0 181.3 %reduce-scatter.11.cloned.1.call-start = ((), (), s32[]{:S(2)}) async-start(), calls=%async_computation.11 | async-start | bytes 3145728 | tf_op jit(solution)/shard_map/reduce_scatter | solution.py:195
  236.8 10.6 %copy-start.4 = (bf16[2,512,8,64]{1,3,2,0:T(8,128)(2,1)S(1)}, bf16[2,512,8,64]{1,3,2,0:T(8,128)(2,1)}, u32[]{:S(2)}) copy-start(bf16[2,512,8,64]{1,3,2,0:T(8,128)(2,1)} %copy-done.3) | copy-start | bytes 3145732
  236.8 10.6 %copy-start.6 = (bf16[2,512,8,64]{1,3,2,0:T(8,128)(2,1)S(1)}, bf16[2,512,8,64]{1,3,2,0:T(8,128)(2,1)}, u32[]{:S(2)}) copy-start(bf16[2,512,8,64]{1,3,2,0:T(8,128)(2,1)} %copy-done.5) | copy-start | bytes 3145732
  236.8 10.6 %copy-start.8 = (bf16[2,512,8,64]{1,3,2,0:T(8,128)(2,1)S(1)}, bf16[2,512,8,64]{1,3,2,0:T(8,128)(2,1)}, u32[]{:S(2)}) copy-start(bf16[2,512,8,64]{1,3,2,0:T(8,128)(2,1)} %copy-done.7) | copy-start | bytes 3145732
  236.8 10.6 %copy-start.37 = (f32[2,8,512]{2,1,0:T(8,128)S(1)}, f32[2,8,512]{2,1,0:T(8,128)}, u32[]{:S(2)}) copy-start(f32[2,8,512]{2,1,0:T(8,128)} %copy-done.36) | copy-start | bytes 98308
  247.5 1.5 copy-start.13
  250.6 2.3 copy-start.14
  252.9 2.6 copy-start.23
  255.5 1.4 copy-start.16
  258.9 1.5 copy-start.13
  261.9 2.3 copy-start.14
  264.3 2.6 copy-start.23
  266.9 1.4 copy-start.16
  270.5 2.7 copy-start.15
  270.5 4.1 copy-start.18
  273.2 2.7 copy-start.32
  273.2 2.7 copy-start.56
  276.0 1.6 copy-start.57
  281.6 366.4 %all-reduce.5.cloned.1.call-start = ((), (), s32[]{:S(2)}) async-start(), calls=%async_computation.13 | async-start | bytes 23068672 | tf_op jit(solution)/shard_map/psum | solution.py:220
  282.1 9.5 %copy-start.54 = (bf16[1024,1024]{1,0:T(8,128)(2,1)S(1)}, bf16[1024,1024]{1,0:T(8,128)(2,1)}, u32[]{:S(2)}) copy-start(bf16[1024,1024]{1,0:T(8,128)(2,1)} %all-gather.9.cloned.1.call-done) | copy-start | bytes 6291460
  282.1 9.5 %copy-start.59 = (bf16[1024,2048]{1,0:T(8,128)(2,1)S(1)}, bf16[1024,2048]{1,0:T(8,128)(2,1)}, u32[]{:S(2)}) copy-start(bf16[1024,2048]{1,0:T(8,128)(2,1)} %copy-done.58) | copy-start | bytes 12582916
  291.6 6.3 copy-start.20
  291.7 6.3 copy-start.55
  297.9 2.3 copy-start.53
  300.2 2.3 copy-start.33
  304.8 4.4 copy-start.38
  304.8 4.4 copy-start.39
  304.8 4.4 copy-start.40
  304.8 50.6 %copy-start.42 = (bf16[2048]{0:T(1024)(128)(2,1)S(1)}, bf16[2048]{0:T(1024)(128)(2,1)}, u32[]{:S(2)}) copy-start(bf16[2048]{0:T(1024)(128)(2,1)} %get-tuple-element.213) | copy-start | bytes 12292
  304.8 97.4 %copy-start.11 = (f32[512,1024]{1,0:T(8,128)S(1)}, f32[512,1024]{1,0:T(8,128)}, u32[]{:S(2)}) copy-start(f32[512,1024]{1,0:T(8,128)} %copy-done.10) | copy-start | bytes 6291460
  304.8 535.9 %all-gather.15.cloned.1.call-start = ((), (), s32[]{:S(2)}) async-start(), calls=%async_computation.12 | async-start | bytes 17825792 | tf_op jit(solution)/shard_map/all_gather | solution.py:216
  648.0 5.8 copy-start.30
  648.0 7.4 copy-start.22
  655.4 4.8 copy-start.21
  840.8 10.7 %copy-start.1 = (bf16[1024,1024]{1,0:T(8,128)(2,1)S(1)}, bf16[1024,1024]{1,0:T(8,128)(2,1)}, u32[]{:S(2)}) copy-start(bf16[1024,1024]{1,0:T(8,128)(2,1)} %param.30) | copy-start | bytes 6291460
  (16 other events, 16.9 us)
Sparse Core Ops, SparseCore 0:
  28.2 13.2 all-gather.6
  84.3 13.2 reduce-scatter.4
  102.0 11.8 all-gather.8
  147.3 13.1 reduce-scatter.6
  169.8 11.8 all-gather.10
  201.4 13.1 reduce-scatter.8
  221.1 11.8 all-gather.12
  281.7 10.7 reduce-scatter.10
  304.9 343.0 all-reduce.4
  650.6 190.1 all-gather.14
